TPU v7x, 32 devices: a whole 2x2x4 slice. The times are simulated.
32 devices in a mesh: ja: 8 (over z, y), pt: 4 (over x, core).
Axes of the slice: x: 2, y: 2, z: 4, core: 2. Of those that a mesh axis runs over, the one named last changes fastest.
Arguments:
- amplitudes: bfloat16 [8, 4, 3072, 512], P('ja', 'pt'), may hold values from -6 to 6
- live_rows: int32 [8, 4], P('ja', 'pt'), may hold values from 384 to 3072, as said below
- hole_coupling: bfloat16 [8, 4, 3, 512, 512], P('ja', 'pt'), may hold values from -0.25 to 0.25
- part_hole: bfloat16 [8, 4, 3072, 512], P('ja', 'pt'), may hold values from -0.0048828125 to 0.0048828125
- recoupling: float32 [8, 3], replicated, may hold values from -1 to 1
Outputs:
- operator_bar: bfloat16 [8, 4, 3072, 512], P('ja', 'pt')
Inputs may be any that keep to these rules, and one draw needn't show every extreme that they name: `live_rows`: rows in use of a channel; some channel has exactly 3072.
All inputs are finite; a program needn't handle non-finite values.
Results may differ from a plain program's by a relative error of at most 0.0085.
Values may be sent and summed in bfloat16 or wider, within the bound.
A program may use at most 128 MiB of HBM per device.

v0:
```python
import functools

import jax
import jax.numpy as jnp
from jax import lax
from jax.experimental import pallas as pl
from jax.experimental.pallas import tpu as pltpu
from jax.sharding import PartitionSpec as P

MESH = pl.DeviceIdType.MESH
CHUNK = 128
BLOCK = 512
HEAD = 4
GAP = 2


def kernel(
    half, chunk, block, head,
    wts, live, amp_hbm, hole_hbm, part_hbm, out,
    amp, hole, part, acc, inter, mix_in, mix, early,
    far_out, far_in, near_out, near_in, side_out, side_in, near_p, side_p,
    amp_sem, part_sem, hole_sem,
    far_s, far_r, near_s, near_r, side_s, side_r, mix_s, mix_r,
):
    rows, holes = amp.shape
    terms = rows // chunk
    mixes = holes // chunk
    total = terms + mixes
    blocks = rows // block
    split = holes - chunk

    chan = lax.axis_index("ja")
    label = lax.axis_index("pt")
    pos = lax.rem(chan, half)
    base = chan - pos
    odd = lax.rem(chan, 2)
    near = chan + 1 - 2 * odd
    far_to = base + lax.rem(pos + half - 2 + 4 * odd, half)
    far_from = base + lax.rem(pos + half + 2 - 4 * odd, half)
    side = label + 2 - 4 * lax.rem(lax.div(label, 2), 2)

    def amp_copy(b):
        part_rows = pl.ds(pl.multiple_of(b * block, block), block)
        return pltpu.make_async_copy(amp_hbm.at[0, 0, part_rows], amp.at[part_rows], amp_sem.at[b])

    def part_copy(b):
        part_rows = pl.ds(pl.multiple_of(b * block, block), block)
        return pltpu.make_async_copy(part_hbm.at[0, 0, part_rows], part.at[part_rows], part_sem.at[b])

    def hole_copy(slot):
        return pltpu.make_async_copy(hole_hbm.at[0, 0, slot], hole.at[slot], hole_sem.at[slot])

    near_slot = 2 - 2 * odd
    far_slot = 2 * odd
    amp_copy(0).start()
    hole_copy(far_slot).start()
    for b in range(blocks):
        if b:
            amp_copy(b).start()
        part_copy(b).start()
    hole_copy(near_slot).start()
    hole_copy(1).start()

    barrier = pltpu.get_barrier_semaphore()
    targets = [{"ja": near}, {"pt": side}, {"ja": far_to}]
    if half != 4:
        targets.append({"ja": far_from})
    for target in targets:
        pl.semaphore_signal(barrier, inc=1, device_id=target, device_id_type=MESH)

    down = jnp.where(pos > 0, wts[0, chan], 0.0)
    up = jnp.where(pos < half - 1, wts[2, chan], 0.0)
    own_w = wts[1, chan]
    near_w = jnp.where(odd == 0, up, down)
    far_w = jnp.where(odd == 0, down, up)
    live_count = live[0, 0]

    def at(k):
        return pl.ds(pl.multiple_of(k * chunk, chunk), chunk)

    def alive(first, count):
        ids = lax.broadcasted_iota(jnp.int32, (count, holes), 0) + first
        return ids < live_count

    def masked(first, count):
        vals = amp[pl.ds(pl.multiple_of(first, count), count)]
        return jnp.where(alive(first, count), vals, jnp.zeros_like(vals))

    def product(j, slot):
        return jnp.dot(masked(j * chunk, chunk), hole[slot], preferred_element_type=jnp.float32)

    def far_copy(k):
        return pltpu.make_async_remote_copy(
            src_ref=far_out.at[at(k)], dst_ref=far_in.at[at(k)],
            send_sem=far_s.at[k], recv_sem=far_r.at[k],
            device_id={"ja": far_to}, device_id_type=MESH,
        )

    def near_copy(k):
        return pltpu.make_async_remote_copy(
            src_ref=near_out.at[at(k)], dst_ref=near_in.at[at(k)],
            send_sem=near_s.at[k], recv_sem=near_r.at[k],
            device_id={"ja": near}, device_id_type=MESH,
        )

    def side_copy(k):
        return pltpu.make_async_remote_copy(
            src_ref=side_out.at[at(k)], dst_ref=side_in.at[at(k)],
            send_sem=side_s.at[k], recv_sem=side_r.at[k],
            device_id={"pt": side}, device_id_type=MESH,
        )

    def mix_copy(m):
        return pltpu.make_async_remote_copy(
            src_ref=inter.at[at(m)], dst_ref=mix_in.at[at(m)],
            send_sem=mix_s.at[m], recv_sem=mix_r.at[m],
            device_id={"pt": side}, device_id_type=MESH,
        )

    def own(k, slot, weight, put):
        @pl.when(k >= terms)
        def _():
            put(weight * mix_in[at(jnp.maximum(k - terms, 0))].astype(jnp.float32))

        @pl.when(k < terms)
        def _():
            put(weight * product(jnp.minimum(k, terms - 1), slot))

    def send_far(k):
        def put(value):
            far_out[at(k)] = value.astype(jnp.bfloat16)

        own(k, far_slot, far_w, put)
        far_copy(k).start()

    def put_near(value):
        near_p[...] = value

    def put_side(value):
        side_p[...] = value

    amp_copy(0).wait()
    hole_copy(far_slot).wait()
    pl.semaphore_wait(barrier, len(targets))

    @pl.loop(0, head)
    def _(k):
        far_out[at(k)] = (far_w * product(k, far_slot)).astype(jnp.bfloat16)
        far_copy(k).start()

    acc[...] = jnp.zeros_like(acc)

    @pl.loop(0, blocks)
    def _(b):
        @pl.when(b > 0)
        def _():
            amp_copy(b).wait()

        part_copy(b).wait()
        first = b * block
        acc[...] += lax.dot_general(
            masked(first, block), part[pl.ds(pl.multiple_of(first, block), block)],
            (((0,), (0,)), ((), ())), preferred_element_type=jnp.float32,
        )

    inter[...] = acc[...].astype(jnp.bfloat16)

    @pl.loop(0, mixes)
    def _(m):
        mix_copy(m).start()

    hole_copy(near_slot).wait()
    hole_copy(1).wait()

    @pl.loop(0, total + GAP)
    def _(t):
        @pl.when(t + head == terms)
        def _():
            for m in range(mixes):
                mix_copy(m).wait_recv()

        @pl.when(t + head < total)
        def _():
            send_far(t + head)

        @pl.when(t < total)
        def _():
            own(t, near_slot, near_w, put_near)

        @pl.when(t >= GAP)
        def _():
            own(jnp.maximum(t - GAP, 0), 1, own_w, put_side)

        @pl.when(t < total)
        def _():
            far_copy(t).wait_recv()
            value = near_p[...] + far_in[at(t)].astype(jnp.float32)
            near_out[at(t)] = value.astype(jnp.bfloat16)
            near_copy(t).start()

        @pl.when(t >= GAP)
        def _():
            k = jnp.maximum(t - GAP, 0)
            near_copy(k).wait_recv()
            value = (side_p[...] + near_in[at(k)].astype(jnp.float32)).astype(jnp.bfloat16)

            @pl.when(k < terms)
            def _():
                j = jnp.minimum(k, terms - 1)
                side_out[at(j)] = value
                side_copy(j).start()

            @pl.when(k >= terms)
            def _():
                mix[at(jnp.maximum(k - terms, 0))] = value

        @pl.when(t == total + GAP - 2)
        def _():
            @pl.loop(0, blocks)
            def _(b):
                where = pl.ds(pl.multiple_of(b * block, block), block)
                early[where] = jnp.dot(
                    amp[where, :split], mix[:split], preferred_element_type=jnp.float32
                )

    @pl.loop(0, blocks)
    def _(b):
        for c in range(block // chunk):
            side_copy(b * (block // chunk) + c).wait_recv()
        where = pl.ds(pl.multiple_of(b * block, block), block)
        value = early[where] + side_in[where].astype(jnp.float32)
        value = value + jnp.dot(
            amp[where, split:], mix[split:], preferred_element_type=jnp.float32
        )
        value = jnp.where(alive(b * block, block), value, jnp.zeros_like(value))
        out[0, 0, where] = value.astype(jnp.bfloat16)

    @pl.loop(0, total)
    def _(k):
        far_copy(k).wait_send()
        near_copy(k).wait_send()

    @pl.loop(0, terms)
    def _(k):
        side_copy(k).wait_send()

    @pl.loop(0, mixes)
    def _(m):
        mix_copy(m).wait_send()


def shards(half, amplitudes, live_rows, hole_coupling, part_hole, recoupling):
    rows, holes = amplitudes.shape[2:]
    chunk, block = min(CHUNK, holes), min(BLOCK, rows)
    total = (rows + holes) // chunk
    terms = rows // chunk
    bf = jnp.bfloat16
    stream = pltpu.VMEM((rows + holes, holes), bf)
    sems = pltpu.SemaphoreType.DMA
    flops = 10 * rows * holes * holes
    return pl.pallas_call(
        functools.partial(kernel, half, chunk, block, min(HEAD, block // chunk)),
        out_shape=pltpu.VMEM(amplitudes.shape, bf),
        in_specs=[pl.BlockSpec(memory_space=pltpu.SMEM)] * 2
        + [pl.BlockSpec(memory_space=pl.ANY)] * 3,
        out_specs=pl.BlockSpec(memory_space=pltpu.VMEM),
        scratch_shapes=[
            pltpu.VMEM((rows, holes), bf),
            pltpu.VMEM((3, holes, holes), bf),
            pltpu.VMEM((rows, holes), bf),
            pltpu.VMEM((holes, holes), jnp.float32),
            pltpu.VMEM((holes, holes), bf),
            pltpu.VMEM((holes, holes), bf),
            pltpu.VMEM((holes, holes), bf),
            pltpu.VMEM((rows, holes), jnp.float32),
            stream, stream, stream, stream,
            pltpu.VMEM((rows, holes), bf),
            pltpu.VMEM((rows, holes), bf),
            pltpu.VMEM((chunk, holes), jnp.float32),
            pltpu.VMEM((chunk, holes), jnp.float32),
            sems((rows // block,)),
            sems((rows // block,)),
            sems((3,)),
            sems((total,)), sems((total,)), sems((total,)), sems((total,)),
            sems((terms,)), sems((terms,)),
            sems((holes // chunk,)), sems((holes // chunk,)),
        ],
        compiler_params=pltpu.CompilerParams(
            collective_id=0, has_side_effects=True, vmem_limit_bytes=60 << 20
        ),
        cost_estimate=pl.CostEstimate(
            flops=flops, bytes_accessed=6 * rows * holes * 2, transcendentals=0
        ),
        name="gt_bar",
    )(recoupling.T, live_rows, amplitudes, hole_coupling, part_hole)


def solution(mesh):
    in_specs = (
        P("ja", "pt", None, None),
        P("ja", "pt"),
        P("ja", "pt", None, None, None),
        P("ja", "pt", None, None),
        P(),
    )
    out_specs = P("ja", "pt", None, None)
    body = functools.partial(shards, mesh.shape["ja"] // 2)
    return jax.shard_map(body, mesh=mesh, in_specs=in_specs, out_specs=out_specs, check_vma=False)
```

profile of v0, /device:TPU:0, one launch (start us, length us, event | category | flops | bytes accessed | tf_op | source)
XLA Modules:
  0.0 97.8 jit_solution(91697394445257518)
XLA Ops:
  0.7 95.5 %gt_bar.1 = bf16[1,1,3072,512]{3,2,1,0:T(8,128)(2,1)S(1)} custom-call(f32[3,8]{1,0:T(4,128)} %bitcast.1, s32[1,1]{1,0:T(1,128)S(6)} %copy.8.live, bf16[1,1,3072,512]{3,2,1,0:T(8,128)(2,1)} %amp_hbm.1, bf16[1,1,3,512,512]{4,3,2,1,0:T(8,128)(2,1)} %hole_hbm.1, bf16[1,1,3072,512]{3,2,1,0:T(8,128)(2,1)} %part_hbm.1), custom_call_target="tpu_custom_call" | custom-call | flops 8053063680 | bytes 18874368 | tf_op jit(solution)/shard_map/gt_bar/pallas_call | solution.py:261
  96.1 1.7 %copy.7 = bf16[1,1,3072,512]{3,2,1,0:T(8,128)(2,1)} copy(bf16[1,1,3072,512]{3,2,1,0:T(8,128)(2,1)S(1)} %gt_bar.1) | data formatting | bytes 6291456
where the time goes:
time: 98 us; the launch traced here: 97.8 us
  Pallas kernels  95.5 us (97%)
  local copies, waits for them, and re-layouts  1.67 us (2%)
    pallas_call x1, Pallas kernels, shards(): pl.pallas_call(functools.partial(kernel, half, chunk, block, min(HEAD, bl...  95.5 us

commit v1 on v0

v1 whole, which is shorter than its diff:
```python
import functools

import jax
import jax.numpy as jnp
from jax import lax
from jax.experimental import pallas as pl
from jax.experimental.pallas import tpu as pltpu
from jax.sharding import PartitionSpec as P

MESH = pl.DeviceIdType.MESH
CHUNK = 128
BLOCK = 512
HEAD = 3
GAP = 2
LAG = 9


def kernel(
    half, chunk, block, raw,
    wts, live, amp_hbm, hole_hbm, part_hbm, out,
    amp, hole, part, acc, inter, mix_in, raw_in, fwd_in, cfar_in, cnear_out, cnear_in, mix,
    far_out, far_in, near_out, near_in, side_out, side_in, near_p, side_p,
    amp_sem, part_sem, hole_sem,
    far_s, far_r, near_s, near_r, side_s, side_r, inter_s, inter_r,
    raw_s, raw_r, fwd_s, fwd_r, cfar_s, cfar_r, cnear_s, cnear_r,
):
    rows, holes = amp.shape
    terms = rows // chunk
    blocks = rows // block
    mixes, _, width = inter.shape
    tail = mixes - raw
    wide = raw * width
    quarter, mid = chunk // 4, chunk // 2
    subs = [(i * quarter, quarter) for i in range(4)] + [(chunk + i * mid, mid) for i in range(2)]
    first_items = {0: range(0, 4), 1: range(4, 6)}

    chans = wts.shape[1]
    chan = lax.axis_index("ja")
    label = lax.axis_index("pt")
    pos = lax.rem(chan, half)
    base = chan - pos
    odd = lax.rem(chan, 2)
    sign = 2 * odd - 1
    near = chan - sign
    has_to = jnp.logical_and(pos + 2 * sign >= 0, pos + 2 * sign < half)
    has_from = jnp.logical_and(pos - 2 * sign >= 0, pos - 2 * sign < half)
    far_to = base + lax.rem(pos + half + 2 * sign, half)
    far_from = base + lax.rem(pos + half - 2 * sign, half)
    side = label + 2 - 4 * lax.rem(lax.div(label, 2), 2)

    near_slot = 2 - 2 * odd
    far_slot = 2 * odd

    def amp_copy(b):
        start, size = b * block, block
        if isinstance(b, int) and b == 0:
            start, size = 2 * chunk, block - 2 * chunk
        part_rows = pl.ds(start, size)
        return pltpu.make_async_copy(amp_hbm.at[0, 0, part_rows], amp.at[part_rows], amp_sem.at[b])

    def head_copy():
        part_rows = pl.ds(0, 2 * chunk)
        return pltpu.make_async_copy(
            amp_hbm.at[0, 0, part_rows], amp.at[part_rows], amp_sem.at[blocks]
        )

    def part_copy(b):
        part_rows = pl.ds(b * block, block)
        return pltpu.make_async_copy(part_hbm.at[0, 0, part_rows], part.at[part_rows], part_sem.at[b])

    def hole_copy(slot):
        return pltpu.make_async_copy(hole_hbm.at[0, 0, slot], hole.at[slot], hole_sem.at[slot])

    head_copy().start()

    @pl.when(has_to)
    def _():
        hole_copy(far_slot).start()

    hole_copy(near_slot).start()
    for b in range(blocks):
        amp_copy(b).start()
        part_copy(b).start()
    hole_copy(1).start()

    barrier = pltpu.get_barrier_semaphore()
    pl.semaphore_signal(barrier, inc=1, device_id={"ja": near}, device_id_type=MESH)
    pl.semaphore_signal(barrier, inc=1, device_id={"pt": side}, device_id_type=MESH)

    @pl.when(has_to)
    def _():
        pl.semaphore_signal(barrier, inc=1, device_id={"ja": far_to}, device_id_type=MESH)

    @pl.when(has_from)
    def _():
        pl.semaphore_signal(barrier, inc=1, device_id={"ja": far_from}, device_id_type=MESH)

    def weight(slot, source, valid):
        clipped = jnp.clip(source, 0, chans - 1)
        return jnp.where(valid, wts[slot, clipped], 0.0)

    def pick(when_odd, when_even, slot_odd, slot_even, valid):
        return jnp.where(
            odd == 1, weight(slot_odd, when_odd, valid), weight(slot_even, when_even, valid)
        )

    always = half > 1
    own_w = wts[1, chan]
    near_w = pick(chan, chan, 0, 2, always)
    far_w = pick(chan, chan, 2, 0, has_to)
    from_near_w = pick(near, near, 2, 0, always)
    from_next_w = pick(chan + 1, chan - 1, 0, 2, has_to)
    from_far_w = pick(chan - 2, chan + 2, 2, 0, has_from)
    live_count = live[0, 0]

    def span(first, count):
        if isinstance(first, int):
            return pl.ds(first, count)
        return pl.ds(pl.multiple_of(first, count), count)

    def at(k):
        return span(k * chunk, chunk)

    def alive(first, count, columns):
        ids = lax.broadcasted_iota(jnp.int32, (count, columns), 0) + first
        return ids < live_count

    def masked(first, count):
        vals = amp[span(first, count)]
        return jnp.where(alive(first, count, holes), vals, jnp.zeros_like(vals))

    def product(k, slot):
        return jnp.dot(amp[at(k)], hole[slot], preferred_element_type=jnp.float32)

    def remote(src, dst, send, recv, target):
        return pltpu.make_async_remote_copy(
            src_ref=src, dst_ref=dst, send_sem=send, recv_sem=recv,
            device_id=target, device_id_type=MESH,
        )

    def item(k):
        return k + 4

    def far_copy(i, where):
        return remote(far_out.at[where], far_in.at[where], far_s.at[i], far_r.at[i], {"ja": far_to})

    def near_copy(i, where):
        return remote(near_out.at[where], near_in.at[where], near_s.at[i], near_r.at[i], {"ja": near})

    def side_copy(k):
        return remote(side_out.at[at(k)], side_in.at[at(k)], side_s.at[k], side_r.at[k], {"pt": side})

    def inter_copy(m):
        return remote(inter.at[m], mix_in.at[m], inter_s.at[m], inter_r.at[m], {"pt": side})

    def raw_copy(m):
        return remote(mix_in.at[m], raw_in.at[m], raw_s.at[m], raw_r.at[m], {"ja": near})

    def fwd_copy(m):
        return remote(raw_in.at[m], fwd_in.at[m], fwd_s.at[m], fwd_r.at[m], {"ja": far_from})

    def cfar_copy(m):
        return remote(mix_in.at[raw + m], cfar_in.at[m], cfar_s.at[m], cfar_r.at[m], {"ja": far_to})

    def cnear_copy(m):
        return remote(cnear_out.at[m], cnear_in.at[m], cnear_s.at[m], cnear_r.at[m], {"ja": near})

    def sub_span(i):
        return pl.ds(*subs[i])

    def chunk_copies(make, k):
        if isinstance(k, int) and k in first_items:
            return [make(i, sub_span(i)) for i in first_items[k]]
        return [make(item(k), at(k))]

    def send_far(k):
        far_out[at(k)] = (far_w * product(k, far_slot)).astype(jnp.bfloat16)
        for copy in chunk_copies(far_copy, k):
            copy.start()

    def send_near(i, where, there):
        @pl.when(has_from)
        def _():
            far_copy(i, where).wait_recv()

        @pl.when(jnp.logical_not(has_from))
        def _():
            far_in[where] = jnp.zeros((there.size, holes), jnp.bfloat16)

        value = near_p[there] + far_in[where].astype(jnp.float32)
        near_out[where] = value.astype(jnp.bfloat16)
        near_copy(i, where).start()

    def send_near_sub(i):
        send_near(i, sub_span(i), sub_span(i))

    def send_side(k):
        side_p[...] = own_w * product(k, 1)
        for copy in chunk_copies(near_copy, k):
            copy.wait_recv()
        value = side_p[...] + near_in[at(k)].astype(jnp.float32)
        side_out[at(k)] = value.astype(jnp.bfloat16)
        side_copy(k).start()

    def finish(first, count, low, high):
        where = span(first, count)
        value = jnp.dot(amp[where], mix[:, low:high], preferred_element_type=jnp.float32)
        value = value + side_in[where, low:high].astype(jnp.float32)
        value = jnp.where(alive(first, count, high - low), value, jnp.zeros_like(value))
        out[0, 0, where, low:high] = value.astype(jnp.bfloat16)

    head_copy().wait()
    amp[pl.ds(0, 2 * chunk)] = masked(0, 2 * chunk)

    @pl.when(has_to)
    def _():
        hole_copy(far_slot).wait()

    pl.semaphore_wait(barrier, 2 + has_to.astype(jnp.int32) + has_from.astype(jnp.int32))

    @pl.when(has_to)
    def _():
        send_far(0)
        send_far(1)

    hole_copy(near_slot).wait()
    for k in range(2):
        near_p[at(k)] = near_w * product(k, near_slot)

    def late_far(k):
        @pl.when(has_to)
        def _():
            send_far(k)

    def gather(b):
        amp_copy(b).wait()
        part_copy(b).wait()
        value = masked(b * block, block)
        amp[span(b * block, block)] = value
        value = lax.dot_general(
            value, part[span(b * block, block)],
            (((0,), (0,)), ((), ())), preferred_element_type=jnp.float32,
        )
        acc[...] = value if b == 0 else acc[...] + value

    between = {0: (), 1: (), 2: (0, 1), 3: (2, 3), 4: (4,)}
    for b in range(blocks):
        gather(b)
        for i in between.get(b, ()):
            send_near_sub(i)
        if b < 3:
            late_far(2 + b)

    for m in range(mixes):
        inter[m] = acc[:, m * width:(m + 1) * width].astype(jnp.bfloat16)
        inter_copy(m).start()
    sent = {i for b in range(blocks) for i in between.get(b, ())}
    for i in range(len(subs)):
        if i not in sent:
            send_near_sub(i)
    hole_copy(1).wait()

    def step(t, far=True, finishing=False):
        if far:
            late_far(t + HEAD)
        near_p[:chunk] = near_w * product(t, near_slot)
        send_near(item(t), at(t), pl.ds(0, chunk))
        send_side(t - GAP)
        if finishing:
            k = t - LAG
            side_copy(k).wait_recv()
            finish(k * chunk, chunk, 0, wide)

    for m in range(raw):
        inter_copy(m).wait_recv()
        raw_copy(m).start()
    step(2)
    step(3)
    for m in range(raw):
        raw_copy(m).wait_recv()

        @pl.when(has_from)
        def _():
            fwd_copy(m).start()

    for m in range(raw, mixes):
        inter_copy(m).wait_recv()

    pl.loop(4, LAG)(step)

    for m in range(raw):
        @pl.when(has_to)
        def _():
            fwd_copy(m).wait_recv()

        @pl.when(jnp.logical_not(has_to))
        def _():
            fwd_in[m] = jnp.zeros((holes, width), jnp.bfloat16)

        value = own_w * mix_in[m].astype(jnp.float32)
        value = value + from_near_w * raw_in[m].astype(jnp.float32)
        value = value + from_next_w * fwd_in[m].astype(jnp.float32)
        mix[:, m * width:(m + 1) * width] = value.astype(jnp.bfloat16)

    pl.loop(LAG, terms - HEAD)(functools.partial(step, finishing=True))

    for m in range(tail):
        @pl.when(has_to)
        def _():
            cfar_copy(m).start()

    pl.loop(terms - HEAD, terms)(functools.partial(step, far=False, finishing=True))

    for m in range(tail):
        @pl.when(has_from)
        def _():
            cfar_copy(m).wait_recv()

        @pl.when(jnp.logical_not(has_from))
        def _():
            cfar_in[m] = jnp.zeros((holes, width), jnp.bfloat16)

        value = near_w * mix_in[raw + m].astype(jnp.float32)
        value = value + from_far_w * cfar_in[m].astype(jnp.float32)
        cnear_out[m] = value.astype(jnp.bfloat16)
        cnear_copy(m).start()

    for k in range(terms - GAP, terms):
        send_side(k)

    def finish_chunk(k):
        side_copy(k).wait_recv()
        finish(k * chunk, chunk, 0, wide)

    pl.loop(terms - LAG, terms - 2)(finish_chunk)

    for m in range(tail):
        low = wide + m * width
        high = low + width
        cnear_copy(m).wait_recv()
        value = own_w * mix_in[raw + m].astype(jnp.float32) + cnear_in[m].astype(jnp.float32)
        mix[:, low:high] = value.astype(jnp.bfloat16)

        @pl.loop(0, blocks - 1)
        def _(b):
            finish(b * block, block, low, high)

        if m == 0:
            finish_chunk(terms - 2)

            @pl.when(has_to)
            def _():
                for k in range(2):
                    for copy in chunk_copies(far_copy, k):
                        copy.wait_send()

                @pl.loop(2, terms)
                def _(k):
                    far_copy(item(k), at(k)).wait_send()

                for n in range(tail):
                    cfar_copy(n).wait_send()

            @pl.when(has_from)
            def _():
                for n in range(raw):
                    fwd_copy(n).wait_send()

            for n in range(mixes):
                inter_copy(n).wait_send()
            for n in range(raw):
                raw_copy(n).wait_send()

    finish_chunk(terms - 1)
    finish((blocks - 1) * block, block, wide, holes)

    for k in range(2):
        for copy in chunk_copies(near_copy, k):
            copy.wait_send()

    @pl.loop(2, terms)
    def _(k):
        near_copy(item(k), at(k)).wait_send()

    @pl.loop(0, terms)
    def _(k):
        side_copy(k).wait_send()

    for n in range(tail):
        cnear_copy(n).wait_send()


def shards(half, amplitudes, live_rows, hole_coupling, part_hole, recoupling):
    rows, holes = amplitudes.shape[2:]
    chunk, block = min(CHUNK, holes), min(BLOCK, rows)
    width = min(128, holes)
    mixes = holes // width
    raw = mixes // 2
    tail = mixes - raw
    terms = rows // chunk
    bf = jnp.bfloat16
    stream = pltpu.VMEM((rows, holes), bf)

    def panels(count):
        return pltpu.VMEM((count, holes, width), bf)

    sems = pltpu.SemaphoreType.DMA
    flops = 10 * rows * holes * holes
    return pl.pallas_call(
        functools.partial(kernel, half, chunk, block, raw),
        out_shape=pltpu.VMEM(amplitudes.shape, bf),
        in_specs=[pl.BlockSpec(memory_space=pltpu.SMEM)] * 2
        + [pl.BlockSpec(memory_space=pl.ANY)] * 3,
        out_specs=pl.BlockSpec(memory_space=pltpu.VMEM),
        scratch_shapes=[
            pltpu.VMEM((rows, holes), bf),
            pltpu.VMEM((3, holes, holes), bf),
            pltpu.VMEM((rows, holes), bf),
            pltpu.VMEM((holes, holes), jnp.float32),
            panels(mixes), panels(mixes), panels(raw), panels(raw),
            panels(tail), panels(tail), panels(tail),
            pltpu.VMEM((holes, holes), bf),
            stream, stream, stream, stream, stream, stream,
            pltpu.VMEM((2 * chunk, holes), jnp.float32),
            pltpu.VMEM((chunk, holes), jnp.float32),
            sems((rows // block + 1,)),
            sems((rows // block,)),
            sems((3,)),
            sems((terms + 4,)), sems((terms + 4,)), sems((terms + 4,)), sems((terms + 4,)),
            sems((terms,)), sems((terms,)),
            sems((mixes,)), sems((mixes,)),
            sems((raw,)), sems((raw,)), sems((raw,)), sems((raw,)),
            sems((tail,)), sems((tail,)), sems((tail,)), sems((tail,)),
        ],
        compiler_params=pltpu.CompilerParams(
            collective_id=0, has_side_effects=True, vmem_limit_bytes=60 << 20
        ),
        cost_estimate=pl.CostEstimate(
            flops=flops, bytes_accessed=6 * rows * holes * 2, transcendentals=0
        ),
        name="gt_bar",
    )(recoupling.T, live_rows, amplitudes, hole_coupling, part_hole)


def solution(mesh):
    in_specs = (
        P("ja", "pt", None, None),
        P("ja", "pt"),
        P("ja", "pt", None, None, None),
        P("ja", "pt", None, None),
        P(),
    )
    out_specs = P("ja", "pt", None, None)
    body = functools.partial(shards, mesh.shape["ja"] // 2)
    return jax.shard_map(body, mesh=mesh, in_specs=in_specs, out_specs=out_specs, check_vma=False)
```

time: 98 us -> 97 us (0.990)
  Pallas kernels: 95.5 us -> 94.5 us
where the time goes in v1:
time: 97 us; the launch traced here: 96.9 us
  Pallas kernels  94.5 us (97%)
  local copies, waits for them, and re-layouts  1.67 us (2%)
    pallas_call x1, Pallas kernels, shards(): pl.pallas_call(functools.partial(kernel, half, chunk, block, raw), out_sh...  94.5 us

profile of v1, /device:TPU:0, one launch (start us, length us, event | category | flops | bytes accessed | tf_op | source)
XLA Modules:
  0.0 96.9 jit_solution(3658487502585232293)
XLA Ops:
  0.7 94.5 %gt_bar.1 = bf16[1,1,3072,512]{3,2,1,0:T(8,128)(2,1)S(1)} custom-call(f32[3,8]{1,0:T(4,128)} %bitcast.1, s32[1,1]{1,0:T(1,128)S(6)} %copy.8.live, bf16[1,1,3072,512]{3,2,1,0:T(8,128)(2,1)} %amp_hbm.1, bf16[1,1,3,512,512]{4,3,2,1,0:T(8,128)(2,1)} %hole_hbm.1, bf16[1,1,3072,512]{3,2,1,0:T(8,128)(2,1)} %part_hbm.1), custom_call_target="tpu_custom_call" | custom-call | flops 8053063680 | bytes 18874368 | tf_op jit(solution)/shard_map/gt_bar/pallas_call | solution.py:409
  95.2 1.7 %copy.7 = bf16[1,1,3072,512]{3,2,1,0:T(8,128)(2,1)} copy(bf16[1,1,3072,512]{3,2,1,0:T(8,128)(2,1)S(1)} %gt_bar.1) | data formatting | bytes 6291456

commit v2 on v1

--- a/solution.py
+++ b/solution.py
@@ -10,13 +10,14 @@
 MESH = pl.DeviceIdType.MESH
 CHUNK = 128
 BLOCK = 512
+GATHER = 1024
 HEAD = 3
 GAP = 2
 LAG = 9
 
 
 def kernel(
-    half, chunk, block, raw,
+    half, chunk, block, gather_rows, raw,
     wts, live, amp_hbm, hole_hbm, part_hbm, out,
     amp, hole, part, acc, inter, mix_in, raw_in, fwd_in, cfar_in, cnear_out, cnear_in, mix,
     far_out, far_in, near_out, near_in, side_out, side_in, near_p, side_p,
@@ -27,6 +28,7 @@
     rows, holes = amp.shape
     terms = rows // chunk
     blocks = rows // block
+    gathers = rows // gather_rows
     mixes, _, width = inter.shape
     tail = mixes - raw
     wide = raw * width
@@ -52,20 +54,20 @@
     far_slot = 2 * odd
 
     def amp_copy(b):
-        start, size = b * block, block
-        if isinstance(b, int) and b == 0:
-            start, size = 2 * chunk, block - 2 * chunk
+        start, size = b * gather_rows, gather_rows
+        if b == 0:
+            start, size = 2 * chunk, gather_rows - 2 * chunk
         part_rows = pl.ds(start, size)
         return pltpu.make_async_copy(amp_hbm.at[0, 0, part_rows], amp.at[part_rows], amp_sem.at[b])
 
     def head_copy():
         part_rows = pl.ds(0, 2 * chunk)
         return pltpu.make_async_copy(
-            amp_hbm.at[0, 0, part_rows], amp.at[part_rows], amp_sem.at[blocks]
+            amp_hbm.at[0, 0, part_rows], amp.at[part_rows], amp_sem.at[gathers]
         )
 
     def part_copy(b):
-        part_rows = pl.ds(b * block, block)
+        part_rows = pl.ds(b * gather_rows, gather_rows)
         return pltpu.make_async_copy(part_hbm.at[0, 0, part_rows], part.at[part_rows], part_sem.at[b])
 
     def hole_copy(slot):
@@ -78,7 +80,7 @@
         hole_copy(far_slot).start()
 
     hole_copy(near_slot).start()
-    for b in range(blocks):
+    for b in range(gathers):
         amp_copy(b).start()
         part_copy(b).start()
     hole_copy(1).start()
@@ -126,8 +128,7 @@
         return ids < live_count
 
     def masked(first, count):
-        vals = amp[span(first, count)]
-        return jnp.where(alive(first, count, holes), vals, jnp.zeros_like(vals))
+        return amp[span(first, count)] * alive(first, count, 1).astype(jnp.bfloat16)
 
     def product(k, slot):
         return jnp.dot(amp[at(k)], hole[slot], preferred_element_type=jnp.float32)
@@ -190,9 +191,6 @@
         value = near_p[there] + far_in[where].astype(jnp.float32)
         near_out[where] = value.astype(jnp.bfloat16)
         near_copy(i, where).start()
-
-    def send_near_sub(i):
-        send_near(i, sub_span(i), sub_span(i))
 
     def send_side(k):
         side_p[...] = own_w * product(k, 1)
@@ -227,37 +225,48 @@
     for k in range(2):
         near_p[at(k)] = near_w * product(k, near_slot)
 
+    @pl.when(jnp.logical_not(has_from))
+    def _():
+        for i in range(len(subs)):
+            where = sub_span(i)
+            near_out[where] = near_p[where].astype(jnp.bfloat16)
+            near_copy(i, where).start()
+
     def late_far(k):
         @pl.when(has_to)
         def _():
             send_far(k)
 
-    def gather(b):
+    for b in range(gathers):
         amp_copy(b).wait()
         part_copy(b).wait()
-        value = masked(b * block, block)
-        amp[span(b * block, block)] = value
+        where = pl.ds(b * gather_rows, gather_rows)
+        value = masked(b * gather_rows, gather_rows)
+        amp[where] = value
         value = lax.dot_general(
-            value, part[span(b * block, block)],
-            (((0,), (0,)), ((), ())), preferred_element_type=jnp.float32,
+            value, part[where], (((0,), (0,)), ((), ())), preferred_element_type=jnp.float32,
         )
-        acc[...] = value if b == 0 else acc[...] + value
-
-    between = {0: (), 1: (), 2: (0, 1), 3: (2, 3), 4: (4,)}
-    for b in range(blocks):
-        gather(b)
-        for i in between.get(b, ()):
-            send_near_sub(i)
-        if b < 3:
-            late_far(2 + b)
-
-    for m in range(mixes):
-        inter[m] = acc[:, m * width:(m + 1) * width].astype(jnp.bfloat16)
-        inter_copy(m).start()
-    sent = {i for b in range(blocks) for i in between.get(b, ())}
+        if b:
+            value = acc[...] + value
+        if b < gathers - 1:
+            acc[...] = value
+            continue
+        for m in range(mixes):
+            inter[m] = value[:, m * width:(m + 1) * width].astype(jnp.bfloat16)
+            inter_copy(m).start()
+
+    early = {1: (2,), 3: (3,), 4: (4,)}
     for i in range(len(subs)):
-        if i not in sent:
-            send_near_sub(i)
+        @pl.when(has_from)
+        def _():
+            where = sub_span(i)
+            far_copy(i, where).wait_recv()
+            value = near_p[where] + far_in[where].astype(jnp.float32)
+            near_out[where] = value.astype(jnp.bfloat16)
+            near_copy(i, where).start()
+
+        for k in early.get(i, ()):
+            late_far(k)
     hole_copy(1).wait()
 
     def step(t, far=True, finishing=False):
@@ -393,6 +402,7 @@
 def shards(half, amplitudes, live_rows, hole_coupling, part_hole, recoupling):
     rows, holes = amplitudes.shape[2:]
     chunk, block = min(CHUNK, holes), min(BLOCK, rows)
+    gather = min(GATHER, rows)
     width = min(128, holes)
     mixes = holes // width
     raw = mixes // 2
@@ -407,7 +417,7 @@
     sems = pltpu.SemaphoreType.DMA
     flops = 10 * rows * holes * holes
     return pl.pallas_call(
-        functools.partial(kernel, half, chunk, block, raw),
+        functools.partial(kernel, half, chunk, block, gather, raw),
         out_shape=pltpu.VMEM(amplitudes.shape, bf),
         in_specs=[pl.BlockSpec(memory_space=pltpu.SMEM)] * 2
         + [pl.BlockSpec(memory_space=pl.ANY)] * 3,
@@ -423,8 +433,8 @@
             stream, stream, stream, stream, stream, stream,
             pltpu.VMEM((2 * chunk, holes), jnp.float32),
             pltpu.VMEM((chunk, holes), jnp.float32),
-            sems((rows // block + 1,)),
-            sems((rows // block,)),
+            sems((rows // gather + 1,)),
+            sems((rows // gather,)),
             sems((3,)),
             sems((terms + 4,)), sems((terms + 4,)), sems((terms + 4,)), sems((terms + 4,)),
             sems((terms,)), sems((terms,)),

time: 97 us -> 93.9 us (0.968)
  Pallas kernels: 94.5 us -> 91.4 us
    pallas_call x1, Pallas kernels: 94.5 us -> 91.4 us  [shards(): pl.pallas_call(functools.partial(kernel, half, chunk, block, gather, raw)...]
where the time goes in v2:
time: 93.9 us; the launch traced here: 93.8 us
  Pallas kernels  91.4 us (97%)
  local copies, waits for them, and re-layouts  1.67 us (2%)
    pallas_call x1, Pallas kernels, shards(): pl.pallas_call(functools.partial(kernel, half, chunk, block, gather, raw)...  91.4 us

profile of v2, /device:TPU:0, one launch (start us, length us, event | category | flops | bytes accessed | tf_op | source)
XLA Modules:
  0.0 93.8 jit_solution(2842590125477415740)
XLA Ops:
  0.7 91.4 %gt_bar.1 = bf16[1,1,3072,512]{3,2,1,0:T(8,128)(2,1)S(1)} custom-call(f32[3,8]{1,0:T(4,128)} %bitcast.1, s32[1,1]{1,0:T(1,128)S(6)} %copy.8.live, bf16[1,1,3072,512]{3,2,1,0:T(8,128)(2,1)} %amp_hbm.1, bf16[1,1,3,512,512]{4,3,2,1,0:T(8,128)(2,1)} %hole_hbm.1, bf16[1,1,3072,512]{3,2,1,0:T(8,128)(2,1)} %part_hbm.1), custom_call_target="tpu_custom_call" | custom-call | flops 8053063680 | bytes 18874368 | tf_op jit(solution)/shard_map/gt_bar/pallas_call | solution.py:419
  92.1 1.7 %copy.7 = bf16[1,1,3072,512]{3,2,1,0:T(8,128)(2,1)} copy(bf16[1,1,3072,512]{3,2,1,0:T(8,128)(2,1)S(1)} %gt_bar.1) | data formatting | bytes 6291456

commit v3 on v2

--- a/solution.py
+++ b/solution.py
@@ -14,16 +14,19 @@
 HEAD = 3
 GAP = 2
 LAG = 9
+SWEEPS = 1
 
 
 def kernel(
     half, chunk, block, gather_rows, raw,
     wts, live, amp_hbm, hole_hbm, part_hbm, out,
     amp, hole, part, acc, inter, mix_in, raw_in, fwd_in, cfar_in, cnear_out, cnear_in, mix,
+    ext_in, next_in,
     far_out, far_in, near_out, near_in, side_out, side_in, near_p, side_p,
     amp_sem, part_sem, hole_sem,
     far_s, far_r, near_s, near_r, side_s, side_r, inter_s, inter_r,
     raw_s, raw_r, fwd_s, fwd_r, cfar_s, cfar_r, cnear_s, cnear_r,
+    ext_s, ext_r, next_s, next_r,
 ):
     rows, holes = amp.shape
     terms = rows // chunk
@@ -33,8 +36,12 @@
     tail = mixes - raw
     wide = raw * width
     quarter, mid = chunk // 4, chunk // 2
-    subs = [(i * quarter, quarter) for i in range(4)] + [(chunk + i * mid, mid) for i in range(2)]
-    first_items = {0: range(0, 4), 1: range(4, 6)}
+    subs = [
+        (0, mid), (mid, quarter), (mid + quarter, quarter), (chunk, mid), (chunk + mid, mid)
+    ]
+    first_items = {0: range(0, 3), 1: range(3, 5)}
+    ahead = len(subs) - 2
+    direct = pl.ds(0, mid)
 
     chans = wts.shape[1]
     chan = lax.axis_index("ja")
@@ -140,7 +147,7 @@
         )
 
     def item(k):
-        return k + 4
+        return k + ahead
 
     def far_copy(i, where):
         return remote(far_out.at[where], far_in.at[where], far_s.at[i], far_r.at[i], {"ja": far_to})
@@ -166,12 +173,19 @@
     def cnear_copy(m):
         return remote(cnear_out.at[m], cnear_in.at[m], cnear_s.at[m], cnear_r.at[m], {"ja": near})
 
+    def ext_copy():
+        return remote(far_out.at[direct], ext_in, ext_s.at[0], ext_r.at[0], {"ja": near})
+
+    def next_copy():
+        return remote(ext_in, next_in, next_s.at[0], next_r.at[0], {"ja": far_from})
+
     def sub_span(i):
         return pl.ds(*subs[i])
 
     def chunk_copies(make, k):
         if isinstance(k, int) and k in first_items:
-            return [make(i, sub_span(i)) for i in first_items[k]]
+            lowest = 1 if make is far_copy else 0
+            return [make(i, sub_span(i)) for i in first_items[k] if i >= lowest]
         return [make(item(k), at(k))]
 
     def send_far(k):
@@ -194,6 +208,12 @@
 
     def send_side(k):
         side_p[...] = own_w * product(k, 1)
+        if isinstance(k, int) and k == 0:
+            @pl.when(has_to)
+            def _():
+                next_copy().wait_recv()
+                side_p[direct] = side_p[direct] + next_in[...].astype(jnp.float32)
+
         for copy in chunk_copies(near_copy, k):
             copy.wait_recv()
         value = side_p[...] + near_in[at(k)].astype(jnp.float32)
@@ -225,9 +245,16 @@
     for k in range(2):
         near_p[at(k)] = near_w * product(k, near_slot)
 
+    near_out[direct] = near_p[direct].astype(jnp.bfloat16)
+    near_copy(0, direct).start()
+
+    @pl.when(has_to)
+    def _():
+        ext_copy().start()
+
     @pl.when(jnp.logical_not(has_from))
     def _():
-        for i in range(len(subs)):
+        for i in range(1, len(subs)):
             where = sub_span(i)
             near_out[where] = near_p[where].astype(jnp.bfloat16)
             near_copy(i, where).start()
@@ -255,8 +282,8 @@
             inter[m] = value[:, m * width:(m + 1) * width].astype(jnp.bfloat16)
             inter_copy(m).start()
 
-    early = {1: (2,), 3: (3,), 4: (4,)}
-    for i in range(len(subs)):
+    behind = {1: (2,), 2: (3,), 3: (4,)}
+    for i in range(1, len(subs)):
         @pl.when(has_from)
         def _():
             where = sub_span(i)
@@ -265,8 +292,13 @@
             near_out[where] = value.astype(jnp.bfloat16)
             near_copy(i, where).start()
 
-        for k in early.get(i, ()):
+        for k in behind.get(i, ()):
             late_far(k)
+    @pl.when(has_from)
+    def _():
+        ext_copy().wait_recv()
+        next_copy().start()
+
     hole_copy(1).wait()
 
     def step(t, far=True, finishing=False):
@@ -343,46 +375,32 @@
 
     pl.loop(terms - LAG, terms - 2)(finish_chunk)
 
-    for m in range(tail):
-        low = wide + m * width
-        high = low + width
-        cnear_copy(m).wait_recv()
-        value = own_w * mix_in[raw + m].astype(jnp.float32) + cnear_in[m].astype(jnp.float32)
-        mix[:, low:high] = value.astype(jnp.bfloat16)
-
-        @pl.loop(0, blocks - 1)
-        def _(b):
-            finish(b * block, block, low, high)
-
-        if m == 0:
-            finish_chunk(terms - 2)
-
-            @pl.when(has_to)
-            def _():
-                for k in range(2):
-                    for copy in chunk_copies(far_copy, k):
-                        copy.wait_send()
-
-                @pl.loop(2, terms)
-                def _(k):
-                    far_copy(item(k), at(k)).wait_send()
-
-                for n in range(tail):
-                    cfar_copy(n).wait_send()
-
-            @pl.when(has_from)
-            def _():
-                for n in range(raw):
-                    fwd_copy(n).wait_send()
-
-            for n in range(mixes):
-                inter_copy(n).wait_send()
-            for n in range(raw):
-                raw_copy(n).wait_send()
-
-    finish_chunk(terms - 1)
-    finish((blocks - 1) * block, block, wide, holes)
-
+    finish_chunk(terms - 2)
+
+    @pl.when(has_to)
+    def _():
+        for k in range(2):
+            for copy in chunk_copies(far_copy, k):
+                copy.wait_send()
+
+        @pl.loop(2, terms)
+        def _(k):
+            far_copy(item(k), at(k)).wait_send()
+
+        for n in range(tail):
+            cfar_copy(n).wait_send()
+        ext_copy().wait_send()
+
+    @pl.when(has_from)
+    def _():
+        for n in range(raw):
+            fwd_copy(n).wait_send()
+        next_copy().wait_send()
+
+    for n in range(mixes):
+        inter_copy(n).wait_send()
+    for n in range(raw):
+        raw_copy(n).wait_send()
     for k in range(2):
         for copy in chunk_copies(near_copy, k):
             copy.wait_send()
@@ -391,12 +409,26 @@
     def _(k):
         near_copy(item(k), at(k)).wait_send()
 
-    @pl.loop(0, terms)
+    @pl.loop(0, terms - 2)
     def _(k):
         side_copy(k).wait_send()
 
-    for n in range(tail):
-        cnear_copy(n).wait_send()
+    for m in range(tail):
+        cnear_copy(m).wait_recv()
+        value = own_w * mix_in[raw + m].astype(jnp.float32) + cnear_in[m].astype(jnp.float32)
+        mix[:, wide + m * width:wide + (m + 1) * width] = value.astype(jnp.bfloat16)
+
+    for b in range(SWEEPS):
+        count = (rows - chunk) // SWEEPS
+        finish(b * count, count, wide, holes)
+
+    side_copy(terms - 1).wait_recv()
+    finish((terms - 1) * chunk, chunk, 0, holes)
+
+    for k in range(terms - 2, terms):
+        side_copy(k).wait_send()
+    for m in range(tail):
+        cnear_copy(m).wait_send()
 
 
 def shards(half, amplitudes, live_rows, hole_coupling, part_hole, recoupling):
@@ -430,17 +462,20 @@
             panels(mixes), panels(mixes), panels(raw), panels(raw),
             panels(tail), panels(tail), panels(tail),
             pltpu.VMEM((holes, holes), bf),
+            pltpu.VMEM((chunk // 2, holes), bf),
+            pltpu.VMEM((chunk // 2, holes), bf),
             stream, stream, stream, stream, stream, stream,
             pltpu.VMEM((2 * chunk, holes), jnp.float32),
             pltpu.VMEM((chunk, holes), jnp.float32),
             sems((rows // gather + 1,)),
             sems((rows // gather,)),
             sems((3,)),
-            sems((terms + 4,)), sems((terms + 4,)), sems((terms + 4,)), sems((terms + 4,)),
+            sems((terms + 3,)), sems((terms + 3,)), sems((terms + 3,)), sems((terms + 3,)),
             sems((terms,)), sems((terms,)),
             sems((mixes,)), sems((mixes,)),
             sems((raw,)), sems((raw,)), sems((raw,)), sems((raw,)),
             sems((tail,)), sems((tail,)), sems((tail,)), sems((tail,)),
+            sems((1,)), sems((1,)), sems((1,)), sems((1,)),
         ],
         compiler_params=pltpu.CompilerParams(
             collective_id=0, has_side_effects=True, vmem_limit_bytes=60 << 20

time: 93.9 us -> 92.8 us (0.988)
  Pallas kernels: 91.4 us -> 90.3 us
    pallas_call x1, Pallas kernels: 91.4 us -> 90.3 us  [shards(): pl.pallas_call(functools.partial(kernel, half, chunk, block, gather, raw)...]
where the time goes in v3:
time: 92.8 us; the launch traced here: 92.6 us
  Pallas kernels  90.3 us (97%)
  local copies, waits for them, and re-layouts  1.67 us (2%)
    pallas_call x1, Pallas kernels, shards(): pl.pallas_call(functools.partial(kernel, half, chunk, block, gather, raw)...  90.3 us

profile of v3, /device:TPU:0, one launch (start us, length us, event | category | flops | bytes accessed | tf_op | source)
XLA Modules:
  0.0 92.6 jit_solution(11778625318268028086)
XLA Ops:
  0.7 90.3 %gt_bar.1 = bf16[1,1,3072,512]{3,2,1,0:T(8,128)(2,1)S(1)} custom-call(f32[3,8]{1,0:T(4,128)} %bitcast.1, s32[1,1]{1,0:T(1,128)S(6)} %copy.8.live, bf16[1,1,3072,512]{3,2,1,0:T(8,128)(2,1)} %amp_hbm.1, bf16[1,1,3,512,512]{4,3,2,1,0:T(8,128)(2,1)} %hole_hbm.1, bf16[1,1,3072,512]{3,2,1,0:T(8,128)(2,1)} %part_hbm.1), custom_call_target="tpu_custom_call" | custom-call | flops 8053063680 | bytes 18874368 | tf_op jit(solution)/shard_map/gt_bar/pallas_call | solution.py:451
  90.9 1.7 %copy.7 = bf16[1,1,3072,512]{3,2,1,0:T(8,128)(2,1)} copy(bf16[1,1,3072,512]{3,2,1,0:T(8,128)(2,1)S(1)} %gt_bar.1) | data formatting | bytes 6291456

commit v4 on v3

--- a/solution.py
+++ b/solution.py
@@ -14,13 +14,13 @@
 HEAD = 3
 GAP = 2
 LAG = 9
-SWEEPS = 1
+STEPS = 3
 
 
 def kernel(
     half, chunk, block, gather_rows, raw,
-    wts, live, amp_hbm, hole_hbm, part_hbm, out,
-    amp, hole, part, acc, inter, mix_in, raw_in, fwd_in, cfar_in, cnear_out, cnear_in, mix,
+    wts, live, amp_hbm, hole_hbm, part_hbm, out, amp, late,
+    hole, part, acc, inter, mix_in, raw_in, fwd_in, cfar_in, cnear_out, cnear_in, mix,
     ext_in, next_in,
     far_out, far_in, near_out, near_in, side_out, side_in, near_p, side_p,
     amp_sem, part_sem, hole_sem,
@@ -220,12 +220,14 @@
         side_out[at(k)] = value.astype(jnp.bfloat16)
         side_copy(k).start()
 
-    def finish(first, count, low, high):
-        where = span(first, count)
-        value = jnp.dot(amp[where], mix[:, low:high], preferred_element_type=jnp.float32)
-        value = value + side_in[where, low:high].astype(jnp.float32)
-        value = jnp.where(alive(first, count, high - low), value, jnp.zeros_like(value))
-        out[0, 0, where, low:high] = value.astype(jnp.bfloat16)
+    def finish(k):
+        side_copy(k).wait_recv()
+        where = at(k)
+        value = jnp.dot(amp[where], mix[...], preferred_element_type=jnp.float32)
+        value = value + side_in[where, :wide].astype(jnp.float32)
+        value = jnp.where(alive(k * chunk, chunk, 1), value, jnp.zeros_like(value))
+        out[where, :wide] = value.astype(jnp.bfloat16)
+        out[where, wide:] = side_in[where, wide:]
 
     head_copy().wait()
     amp[pl.ds(0, 2 * chunk)] = masked(0, 2 * chunk)
@@ -308,9 +310,7 @@
         send_near(item(t), at(t), pl.ds(0, chunk))
         send_side(t - GAP)
         if finishing:
-            k = t - LAG
-            side_copy(k).wait_recv()
-            finish(k * chunk, chunk, 0, wide)
+            finish(t - LAG)
 
     for m in range(raw):
         inter_copy(m).wait_recv()
@@ -369,13 +369,9 @@
     for k in range(terms - GAP, terms):
         send_side(k)
 
-    def finish_chunk(k):
-        side_copy(k).wait_recv()
-        finish(k * chunk, chunk, 0, wide)
-
-    pl.loop(terms - LAG, terms - 2)(finish_chunk)
-
-    finish_chunk(terms - 2)
+    pl.loop(terms - LAG, terms - 2)(finish)
+
+    finish(terms - 2)
 
     @pl.when(has_to)
     def _():
@@ -416,19 +412,44 @@
     for m in range(tail):
         cnear_copy(m).wait_recv()
         value = own_w * mix_in[raw + m].astype(jnp.float32) + cnear_in[m].astype(jnp.float32)
-        mix[:, wide + m * width:wide + (m + 1) * width] = value.astype(jnp.bfloat16)
-
-    for b in range(SWEEPS):
-        count = (rows - chunk) // SWEEPS
-        finish(b * count, count, wide, holes)
-
-    side_copy(terms - 1).wait_recv()
-    finish((terms - 1) * chunk, chunk, 0, holes)
+        late[:, m * width:(m + 1) * width] = value.astype(jnp.bfloat16)
+
+    finish(terms - 1)
 
     for k in range(terms - 2, terms):
         side_copy(k).wait_send()
     for m in range(tail):
         cnear_copy(m).wait_send()
+
+
+def closing(steps, live, first, amp, late, out, stage, sems):
+    rows = amp.shape[0]
+    wide = amp.shape[1] - late.shape[1]
+    count = rows // steps
+    live_count = live[0, 0]
+    copies = []
+    for b in range(steps):
+        where = pl.ds(b * count, count)
+        columns = pl.ds(0, wide)
+        copy = pltpu.make_async_copy(
+            first.at[where, columns], out.at[0, 0, where, columns], sems.at[steps + b]
+        )
+        copy.start()
+        copies.append(copy)
+    for b in range(steps):
+        where = pl.ds(b * count, count)
+        value = jnp.dot(amp[where], late[...], preferred_element_type=jnp.float32)
+        value = value + first[where, wide:].astype(jnp.float32)
+        ids = lax.broadcasted_iota(jnp.int32, (count, 1), 0) + b * count
+        value = jnp.where(ids < live_count, value, jnp.zeros_like(value))
+        stage[where] = value.astype(jnp.bfloat16)
+        copy = pltpu.make_async_copy(
+            stage.at[where], out.at[0, 0, where, pl.ds(wide, late.shape[1])], sems.at[b]
+        )
+        copy.start()
+        copies.append(copy)
+    for copy in copies:
+        copy.wait()
 
 
 def shards(half, amplitudes, live_rows, hole_coupling, part_hole, recoupling):
@@ -448,20 +469,23 @@
 
     sems = pltpu.SemaphoreType.DMA
     flops = 10 * rows * holes * holes
-    return pl.pallas_call(
+    first, amp, late = pl.pallas_call(
         functools.partial(kernel, half, chunk, block, gather, raw),
-        out_shape=pltpu.VMEM(amplitudes.shape, bf),
+        out_shape=(
+            pltpu.VMEM((rows, holes), bf),
+            pltpu.VMEM((rows, holes), bf),
+            pltpu.VMEM((holes, tail * width), bf),
+        ),
         in_specs=[pl.BlockSpec(memory_space=pltpu.SMEM)] * 2
         + [pl.BlockSpec(memory_space=pl.ANY)] * 3,
-        out_specs=pl.BlockSpec(memory_space=pltpu.VMEM),
+        out_specs=[pl.BlockSpec(memory_space=pltpu.VMEM)] * 3,
         scratch_shapes=[
-            pltpu.VMEM((rows, holes), bf),
             pltpu.VMEM((3, holes, holes), bf),
             pltpu.VMEM((rows, holes), bf),
             pltpu.VMEM((holes, holes), jnp.float32),
             panels(mixes), panels(mixes), panels(raw), panels(raw),
             panels(tail), panels(tail), panels(tail),
-            pltpu.VMEM((holes, holes), bf),
+            pltpu.VMEM((holes, raw * width), bf),
             pltpu.VMEM((chunk // 2, holes), bf),
             pltpu.VMEM((chunk // 2, holes), bf),
             stream, stream, stream, stream, stream, stream,
@@ -478,13 +502,26 @@
             sems((1,)), sems((1,)), sems((1,)), sems((1,)),
         ],
         compiler_params=pltpu.CompilerParams(
-            collective_id=0, has_side_effects=True, vmem_limit_bytes=60 << 20
+            collective_id=0, has_side_effects=True, vmem_limit_bytes=56 << 20
         ),
         cost_estimate=pl.CostEstimate(
             flops=flops, bytes_accessed=6 * rows * holes * 2, transcendentals=0
         ),
         name="gt_bar",
     )(recoupling.T, live_rows, amplitudes, hole_coupling, part_hole)
+    return pl.pallas_call(
+        functools.partial(closing, STEPS),
+        out_shape=jax.ShapeDtypeStruct(amplitudes.shape, bf),
+        in_specs=[pl.BlockSpec(memory_space=pltpu.SMEM)]
+        + [pl.BlockSpec(memory_space=pltpu.VMEM)] * 3,
+        out_specs=pl.BlockSpec(memory_space=pl.ANY),
+        scratch_shapes=[pltpu.VMEM((rows, tail * width), bf), sems((2 * STEPS,))],
+        compiler_params=pltpu.CompilerParams(vmem_limit_bytes=24 << 20),
+        cost_estimate=pl.CostEstimate(
+            flops=flops // 10, bytes_accessed=2 * rows * holes * 2, transcendentals=0
+        ),
+        name="gt_close",
+    )(live_rows, first, amp, late)
 
 
 def solution(mesh):

time: 92.8 us -> 92 us (level)
  local copies, waits for them, and re-layouts: 1.67 us -> 0 us
    pallas_call x0 -> x1, Pallas kernels: none -> 2.07 us  [shards(): pl.pallas_call(functools.partial(closing, STEPS), out_shape=jax.ShapeDtyp...]
    unnamed x1 -> x0, local copies, waits for them, and re-layouts: 1.67 us -> none
    pallas_call x1, Pallas kernels: 90.3 us -> 89.2 us  [shards(): pl.pallas_call(functools.partial(kernel, half, chunk, block, gather, raw)...]
where the time goes in v4:
time: 92 us; the launch traced here: 91.9 us
  Pallas kernels  91.2 us (99%)
    pallas_call x1, Pallas kernels, shards(): pl.pallas_call(functools.partial(kernel, half, chunk, block, gather, raw)...  89.2 us
    pallas_call x1, Pallas kernels, shards(): pl.pallas_call(functools.partial(closing, STEPS), out_shape=jax.ShapeDtyp...  2.07 us

profile of v4, /device:TPU:0, one launch (start us, length us, event | category | flops | bytes accessed | tf_op | source)
XLA Modules:
  0.0 91.9 jit_solution(5787796870741156418)
XLA Ops:
  0.7 89.2 %gt_bar.1 = (bf16[3072,512]{1,0:T(8,128)(2,1)S(1)}, bf16[3072,512]{1,0:T(8,128)(2,1)S(1)}, bf16[512,256]{1,0:T(8,128)(2,1)S(1)}) custom-call(f32[3,8]{1,0:T(4,128)} %bitcast.1, s32[1,1]{1,0:T(1,128)S(6)} %copy.6.live, bf16[1,1,3072,512]{3,2,1,0:T(8,128)(2,1)} %amp_hbm.1, bf16[1,1,3,512,512]{4,3,2,1,0:T(8,128)(2,1)} %hole_hbm.1, ...), custom_call_target="tpu_custom_call" | custom-call | flops 8053063680 | bytes 18874368 | tf_op jit(solution)/shard_map/gt_bar/pallas_call | solution.py:472
  89.8 2.1 %gt_close.1 = bf16[1,1,3072,512]{3,2,1,0:T(8,128)(2,1)} custom-call(s32[1,1]{1,0:T(1,128)S(6)} %copy.6.live, bf16[3072,512]{1,0:T(8,128)(2,1)S(1)} %get-tuple-element.8.first, bf16[3072,512]{1,0:T(8,128)(2,1)S(1)} %get-tuple-element.9.amp, bf16[512,256]{1,0:T(8,128)(2,1)S(1)} %get-tuple-element.10.late), custom_call_target="tpu_custom_call" | custom-call | flops 805306368 | bytes 6291456 | tf_op jit(solution)/shard_map/gt_close/pallas_call | solution.py:512

commit v5 on v4

--- a/solution.py
+++ b/solution.py
@@ -10,7 +10,7 @@
 MESH = pl.DeviceIdType.MESH
 CHUNK = 128
 BLOCK = 512
-GATHER = 1024
+GATHER = (5, 4, 3)
 HEAD = 3
 GAP = 2
 LAG = 9
@@ -31,7 +31,8 @@
     rows, holes = amp.shape
     terms = rows // chunk
     blocks = rows // block
-    gathers = rows // gather_rows
+    gathers = len(gather_rows)
+    starts = [sum(gather_rows[:b]) for b in range(gathers)]
     mixes, _, width = inter.shape
     tail = mixes - raw
     wide = raw * width
@@ -61,9 +62,9 @@
     far_slot = 2 * odd
 
     def amp_copy(b):
-        start, size = b * gather_rows, gather_rows
+        start, size = starts[b], gather_rows[b]
         if b == 0:
-            start, size = 2 * chunk, gather_rows - 2 * chunk
+            start, size = 2 * chunk, size - 2 * chunk
         part_rows = pl.ds(start, size)
         return pltpu.make_async_copy(amp_hbm.at[0, 0, part_rows], amp.at[part_rows], amp_sem.at[b])
 
@@ -74,7 +75,7 @@
         )
 
     def part_copy(b):
-        part_rows = pl.ds(b * gather_rows, gather_rows)
+        part_rows = pl.ds(starts[b], gather_rows[b])
         return pltpu.make_async_copy(part_hbm.at[0, 0, part_rows], part.at[part_rows], part_sem.at[b])
 
     def hole_copy(slot):
@@ -269,20 +270,28 @@
     for b in range(gathers):
         amp_copy(b).wait()
         part_copy(b).wait()
-        where = pl.ds(b * gather_rows, gather_rows)
-        value = masked(b * gather_rows, gather_rows)
+        where = pl.ds(starts[b], gather_rows[b])
+        value = masked(starts[b], gather_rows[b])
         amp[where] = value
-        value = lax.dot_general(
-            value, part[where], (((0,), (0,)), ((), ())), preferred_element_type=jnp.float32,
-        )
-        if b:
-            value = acc[...] + value
+        def gathered(columns):
+            return lax.dot_general(
+                value, part[where, columns],
+                (((0,), (0,)), ((), ())), preferred_element_type=jnp.float32,
+            )
+
         if b < gathers - 1:
-            acc[...] = value
+            term = gathered(slice(0, holes))
+            acc[...] = acc[...] + term if b else term
             continue
-        for m in range(mixes):
-            inter[m] = value[:, m * width:(m + 1) * width].astype(jnp.bfloat16)
-            inter_copy(m).start()
+        for low, high in ((0, raw), (raw, mixes)):
+            columns = slice(low * width, high * width)
+            term = gathered(columns)
+            if b:
+                term = acc[:, columns] + term
+            for m in range(low, high):
+                first = (m - low) * width
+                inter[m] = term[:, first:first + width].astype(jnp.bfloat16)
+                inter_copy(m).start()
 
     behind = {1: (2,), 2: (3,), 3: (4,)}
     for i in range(1, len(subs)):
@@ -455,7 +464,7 @@
 def shards(half, amplitudes, live_rows, hole_coupling, part_hole, recoupling):
     rows, holes = amplitudes.shape[2:]
     chunk, block = min(CHUNK, holes), min(BLOCK, rows)
-    gather = min(GATHER, rows)
+    gather = [rows * part // 12 for part in GATHER]
     width = min(128, holes)
     mixes = holes // width
     raw = mixes // 2
@@ -491,8 +500,8 @@
             stream, stream, stream, stream, stream, stream,
             pltpu.VMEM((2 * chunk, holes), jnp.float32),
             pltpu.VMEM((chunk, holes), jnp.float32),
-            sems((rows // gather + 1,)),
-            sems((rows // gather,)),
+            sems((len(gather) + 1,)),
+            sems((len(gather),)),
             sems((3,)),
             sems((terms + 3,)), sems((terms + 3,)), sems((terms + 3,)), sems((terms + 3,)),
             sems((terms,)), sems((terms,)),

time: 92 us -> 92 us (level)
  no operation moved by 1% of the time
where the time goes in v5:
time: 92 us; the launch traced here: 91.9 us
  Pallas kernels  91.2 us (99%)
    pallas_call x1, Pallas kernels, shards(): pl.pallas_call(functools.partial(kernel, half, chunk, block, gather, raw)...  89.1 us
    pallas_call x1, Pallas kernels, shards(): pl.pallas_call(functools.partial(closing, STEPS), out_shape=jax.ShapeDtyp...  2.06 us

profile of v5, /device:TPU:0, one launch (start us, length us, event | category | flops | bytes accessed | tf_op | source)
XLA Modules:
  0.0 91.9 jit_solution(1591770050908509322)
XLA Ops:
  0.7 89.1 %gt_bar.1 = (bf16[3072,512]{1,0:T(8,128)(2,1)S(1)}, bf16[3072,512]{1,0:T(8,128)(2,1)S(1)}, bf16[512,256]{1,0:T(8,128)(2,1)S(1)}) custom-call(f32[3,8]{1,0:T(4,128)} %bitcast.1, s32[1,1]{1,0:T(1,128)S(6)} %copy.6.live, bf16[1,1,3072,512]{3,2,1,0:T(8,128)(2,1)} %amp_hbm.1, bf16[1,1,3,512,512]{4,3,2,1,0:T(8,128)(2,1)} %hole_hbm.1, ...), custom_call_target="tpu_custom_call" | custom-call | flops 8053063680 | bytes 18874368 | tf_op jit(solution)/shard_map/gt_bar/pallas_call | solution.py:481
  89.8 2.1 %gt_close.1 = bf16[1,1,3072,512]{3,2,1,0:T(8,128)(2,1)} custom-call(s32[1,1]{1,0:T(1,128)S(6)} %copy.6.live, bf16[3072,512]{1,0:T(8,128)(2,1)S(1)} %get-tuple-element.8.first, bf16[3072,512]{1,0:T(8,128)(2,1)S(1)} %get-tuple-element.9.amp, bf16[512,256]{1,0:T(8,128)(2,1)S(1)} %get-tuple-element.10.late), custom_call_target="tpu_custom_call" | custom-call | flops 805306368 | bytes 6291456 | tf_op jit(solution)/shard_map/gt_close/pallas_call | solution.py:521
